TPU v7x, 32 devices: a whole 2x2x4 slice. The times are simulated.
32 devices in a mesh: rows: 16 (over z, y, x), rep: 2 (over core).
Axes of the slice: x: 2, y: 2, z: 4, core: 2. Of those that a mesh axis runs over, the one named last changes fastest.
Arguments:
- features: bfloat16 [4096, 128], P(('rows', 'rep')), may hold values from -6 to 6
- tile_counts: int32 [4096, 128, 128], P(('rows', 'rep')), may hold values from 0 to 3, as said below
- tile_row: int32 [4096], P(('rows', 'rep')), may hold values from 0 to 1
- tile_col: int32 [4096], P(('rows', 'rep')), may hold values from 0 to 31, as said below
- label_ids: int32 [2048], P(('rows', 'rep')), may hold values from 0 to 4095, as said below
- cotangent: bfloat16 [4096, 256], P(('rows', 'rep')), may hold values from -6 to 6
- self_weight: bfloat16 [128, 256], replicated, may hold values from -0.5 to 0.5
- neigh_weight: bfloat16 [128, 256], replicated, may hold values from -0.5 to 0.5
Outputs:
- activation: bfloat16 [4096, 256], P(('rows', 'rep'))
- grad_features: float32 [4096, 128], P(('rows', 'rep'))
- grad_self: float32 [128, 256], replicated
- grad_neigh: float32 [128, 256], replicated
Inputs may be any that keep to these rules, and one draw needn't show every extreme that they name: `tile_counts`: edge counts of one tile; most entries are zero. `tile_col`: every tile held by a device of rep index c names a column block of the feature rows of some device of rep index c. On each device, at most 16 tiles name column blocks held by devices of one rows index, and exactly 16 do for some rows index. `label_ids`: the ids of one device's 64 labels are distinct and lie among that device's own feature rows.
All inputs are finite; a program needn't handle non-finite values.
Results may differ from a plain program's by a relative error of at most 0.0053.
Values may be sent and summed in bfloat16 or wider, within the bound.
A program may use at most 128 MiB of HBM per device.

v0:
```python
import jax
import jax.numpy as jnp
from jax import lax
from jax.sharding import PartitionSpec as P

edge_moment = 14.0 / 96.0


def derivative(preact, masked):
    sigma = jax.nn.sigmoid(preact)
    return (masked.astype(jnp.float32) * sigma * (1.0 + preact * (1.0 - sigma))).astype(
        jnp.bfloat16
    )


def shards(
    features, tile_counts, tile_row, tile_col, label_ids, cotangent, self_weight, neigh_weight
):
    half_rows, width_in = features.shape
    block_size = tile_counts.shape[1]
    tile_total = tile_counts.shape[0]
    rep_count = lax.axis_size("rep")
    row_count = lax.axis_size("rows")
    per_half = half_rows // block_size
    row_blocks = rep_count * per_half
    scale = (edge_moment * tile_total * rep_count * block_size / row_blocks) ** (-0.5)
    gathered = lax.all_gather(features, "rows", axis=0, tiled=True)
    local_col = tile_col // (rep_count * per_half) * per_half + tile_col % per_half
    panels = gathered.reshape(-1, block_size, width_in)[local_col]
    counts = tile_counts.astype(jnp.bfloat16)
    products = jnp.einsum("tij,tjf->tif", counts, panels, preferred_element_type=jnp.float32)
    owner_table = (tile_row[:, None] == jnp.arange(row_blocks, dtype=jnp.int32)[None, :]).astype(
        jnp.float32
    )
    partial_rows = jnp.einsum(
        "tr,tif->rif", owner_table, products, precision=lax.Precision.HIGHEST
    ).reshape(row_blocks * block_size, width_in)
    local_ids = label_ids % half_rows
    label_mask = jnp.any(
        local_ids[:, None] == jnp.arange(half_rows, dtype=jnp.int32)[None, :], axis=0
    )
    masked = cotangent * label_mask[:, None].astype(jnp.bfloat16)
    rep_place = lax.axis_index("rep")
    neighbour_sum = lax.psum(partial_rows, "rep") * scale
    group_feat, group_masked = (
        lax.all_gather(features, "rep", axis=0, tiled=True),
        lax.all_gather(masked, "rep", axis=0, tiled=True),
    )
    neighbour = neighbour_sum.astype(jnp.bfloat16)
    preact = jnp.dot(group_feat, self_weight, preferred_element_type=jnp.float32) + jnp.dot(
        neighbour, neigh_weight, preferred_element_type=jnp.float32
    )
    activation_all = jax.nn.silu(preact).astype(jnp.bfloat16)
    delta_all = derivative(preact, group_masked)
    back = jnp.einsum(
        "nh,fh->nf", delta_all, neigh_weight, preferred_element_type=jnp.float32
    ).astype(jnp.bfloat16)
    activation = lax.dynamic_slice_in_dim(activation_all, rep_place * half_rows, half_rows, 0)
    delta_own = lax.dynamic_slice_in_dim(delta_all, rep_place * half_rows, half_rows, 0)
    neighbour_own = lax.dynamic_slice_in_dim(neighbour, rep_place * half_rows, half_rows, 0)
    self_part = jnp.einsum("nf,nh->fh", features, delta_own, preferred_element_type=jnp.float32)
    neigh_part = jnp.einsum(
        "nf,nh->fh", neighbour_own, delta_own, preferred_element_type=jnp.float32
    )
    pair_self, pair_neigh = lax.psum((self_part, neigh_part), "rep")
    self_total, neigh_total = lax.psum((pair_self, pair_neigh), "rows")
    grad_scale = float(label_ids.shape[0] * row_count * rep_count) ** (-0.5)
    picked = back.reshape(row_blocks, block_size, width_in)[tile_row]
    col_terms = jnp.einsum(
        "tij,tif->tjf", counts, picked, preferred_element_type=jnp.float32
    ).astype(jnp.bfloat16)
    count = half_rows * lax.axis_size("rows")
    block_count = count // block_size
    placing = (local_col[None, :] == jnp.arange(block_count, dtype=jnp.int32)[:, None]).astype(
        jnp.bfloat16
    )
    summed = jnp.einsum("bt,tif->bif", placing, col_terms, preferred_element_type=jnp.float32)
    scattered = lax.psum_scatter(
        summed.reshape(count, width_in), "rows", scatter_dimension=0, tiled=True
    )
    own_term = jnp.einsum("nh,fh->nf", delta_own, self_weight, preferred_element_type=jnp.float32)
    grad_features = own_term + scale * scattered
    return (activation, grad_features, grad_scale * self_total, grad_scale * neigh_total)


def solution(mesh):
    placed = (
        P(("rows", "rep"), None),
        P(("rows", "rep"), None, None),
        P(("rows", "rep")),
        P(("rows", "rep")),
        P(("rows", "rep")),
        P(("rows", "rep"), None),
        P(),
        P(),
    )
    return jax.shard_map(
        shards,
        mesh=mesh,
        in_specs=placed,
        out_specs=(P(("rows", "rep"), None), P(("rows", "rep"), None), P(), P()),
        check_vma=False,
    )
```

profile of v0, /device:TPU:0, one launch (start us, length us, event | category | flops | bytes accessed | tf_op | source)
XLA Modules:
  0.0 322.9 jit_solution(7102248980317323099)
XLA Ops:
  7.2 0.7 compare_select_fusion.1
  7.9 45.6 %all_gather.10 = bf16[2048,128]{1,0:T(8,128)(2,1)S(1)} all-gather(bf16[128,128]{1,0:T(8,128)(2,1)} %param.8), channel_id=1, replica_groups=mesh['rows'=16,'rep'=2] {'rows'}, dimensions={0}, use_global_device_ids=true | all-gather | bytes 557056 | tf_op jit(solution)/shard_map/all_gather | solution.py:27
  53.5 3.1 gather_fusion
  56.5 11.0 %convolution_bitcast_fusion = f32[128,128,128]{1,2,0:T(8,128)} fusion(bf16[128,128,128]{2,1,0:T(8,128)(2,1)} %gather_fusion, s32[128,128,128]{2,1,0:T(8,128)} %param.9), kind=kOutput, calls=%fused_computation.3 | convolution fusion | flops 538968064 | bytes 20971520 | tf_op jit(solution)/shard_map/tij,tjf->tif/dot_general | solution.py:31
  67.5 9.3 %copy.29 = f32[128,128,128]{2,0,1:T(8,128)} copy(f32[128,128,128]{1,2,0:T(8,128)} %convolution_bitcast_fusion) | data formatting | bytes 16777216 | tf_op jit(solution)/shard_map/tij,tjf->tif/dot_general | solution.py:31
  76.8 6.2 %fusion.13 = f32[2,128,128]{2,0,1:T(2,128)S(1)} fusion(f32[128,128,128]{2,0,1:T(8,128)} %copy.29, s32[128]{0:T(128)S(1)} %copy-done.4), kind=kOutput, calls=%fused_computation.35 | convolution fusion | flops 50331904 | bytes 8520192 | tf_op jit(solution)/shard_map/tr,tif->rif/dot_general | solution.py:35
  83.8 1.9 all_gather.9
  86.0 1.9 all_gather.11
  87.9 9.7 %all-reduce.6.cloned.1.call-done = f32[256,128]{1,0:T(8,128)} async-done(((f32[256,128]{1,0:T(8,128)}), f32[256,128]{1,0:T(8,128)}) %all-reduce.6.cloned.1.call-update) | async-done | bytes 131088 | tf_op jit(solution)/shard_map/psum | solution.py:44
  97.6 0.9 multiply_convert_fusion.1
  98.8 0.9 fusion.3
  99.7 0.9 convolution_bitcast_fusion.1
  100.8 3.0 gather_fusion.1
  103.9 8.3 %convert_bitcast_fusion = bf16[128,128,128]{1,2,0:T(8,128)(2,1)} fusion(bf16[128,128,128]{2,1,0:T(8,128)(2,1)} %gather_fusion.1, s32[128,128,128]{2,1,0:T(8,128)} %param.9), kind=kOutput, calls=%fused_computation.2 | convolution fusion | flops 541065216 | bytes 16777216 | tf_op jit(solution)/shard_map/tij,tif->tjf/dot_general | solution.py:69
  112.2 6.7 %copy.32 = bf16[128,128,128]{2,0,1:T(8,128)(2,1)} copy(bf16[128,128,128]{1,2,0:T(8,128)(2,1)} %convert_bitcast_fusion) | data formatting | bytes 8388608 | tf_op jit(solution)/shard_map/convert_element_type | solution.py:71
  118.9 1.5 all-reduce.10.cloned.1.call-done
  120.5 2.8 fusion.10
  123.4 1.3 copy.33
  125.3 109.8 %all-reduce.8.cloned.1.call-done = (f32[128,256]{0,1:T(8,128)}, f32[128,256]{0,1:T(8,128)}) async-done(((f32[128,256]{0,1:T(8,128)}, f32[128,256]{0,1:T(8,128)}), (f32[128,256]{0,1:T(8,128)}, f32[128,256]{0,1:T(8,128)})) %all-reduce.8.cloned.1.call-update) | async-done | bytes 262160 | tf_op jit(solution)/shard_map/psum | solution.py:66
  235.1 1.0 broadcast_multiply_fusion
  236.1 0.8 copy.35
  236.9 0.8 copy.36
  237.6 77.1 %reduce-scatter.2.cloned.1.call-done = f32[128,128]{1,0:T(8,128)} async-done(((f32[2048,128]{1,0:T(8,128)}), f32[128,128]{1,0:T(8,128)}) %reduce-scatter.2.cloned.1.call-update) | async-done | bytes 65552 | tf_op jit(solution)/shard_map/reduce_scatter | solution.py:78
  314.8 1.6 convolution_add_fusion.1
  (32 shorter events, 2.4 us)
Async XLA Ops:
  7.2 91.4 %copy-start = (bf16[128,256]{1,0:T(8,128)(2,1)S(1)}, bf16[128,256]{1,0:T(8,128)(2,1)}, u32[]{:S(2)}) copy-start(bf16[128,256]{1,0:T(8,128)(2,1)} %param.15) | copy-start | bytes 196612
  7.2 90.5 %all-reduce.6.cloned.1.call-start = ((), (), s32[]{:S(2)}) async-start(), calls=%async_computation.1 | async-start | bytes 262144 | tf_op jit(solution)/shard_map/psum | solution.py:44
  67.5 9.3 %copy-start.4 = (s32[128]{0:T(128)S(1)}, s32[128]{0:T(128)}, u32[]{:S(2)}) copy-start(s32[128]{0:T(128)} %param.10) | copy-start | bytes 1540
  76.8 7.0 %copy-start.1 = (bf16[128,128]{1,0:T(8,128)(2,1)S(1)}, bf16[128,128]{1,0:T(8,128)(2,1)}, u32[]{:S(2)}) copy-start(bf16[128,128]{1,0:T(8,128)(2,1)} %param.8) | copy-start | bytes 98308
  76.8 8.9 %copy-start.5 = (s32[64]{0:T(128)S(1)}, s32[64]{0:T(128)}, u32[]{:S(2)}) copy-start(s32[64]{0:T(128)} %param.12) | copy-start | bytes 772
  76.8 9.0 %copy-start.2 = (bf16[128,256]{1,0:T(8,128)(2,1)S(1)}, bf16[128,256]{1,0:T(8,128)(2,1)}, u32[]{:S(2)}) copy-start(bf16[128,256]{1,0:T(8,128)(2,1)} %param.14) | copy-start | bytes 196612
  76.8 9.1 %copy-start.3 = (bf16[128,256]{1,0:T(8,128)(2,1)S(1)}, bf16[128,256]{1,0:T(8,128)(2,1)}, u32[]{:S(2)}) copy-start(bf16[128,256]{1,0:T(8,128)(2,1)} %param.13) | copy-start | bytes 196612
  83.7 36.7 %all-reduce.10.cloned.1.call-start = ((), (), s32[]{:S(2)}) async-start(), calls=%async_computation.4 | async-start | bytes 524288 | tf_op jit(solution)/shard_map/psum | solution.py:65
  100.8 134.3 %all-reduce.8.cloned.1.call-start = ((), (), s32[]{:S(2)}) async-start(), calls=%async_computation.3 | async-start | bytes 524288 | tf_op jit(solution)/shard_map/psum | solution.py:66
  120.5 194.3 %reduce-scatter.2.cloned.1.call-start = ((), (), s32[]{:S(2)}) async-start(), calls=%async_computation.2 | async-start | bytes 1114112 | tf_op jit(solution)/shard_map/reduce_scatter | solution.py:78
Sparse Core Ops, SparseCore 0:
  83.8 13.7 all-reduce.5
  100.9 19.4 all-reduce.9
  125.7 109.3 all-reduce.7
  237.2 77.4 reduce-scatter.1
where the time goes:
time: 323 us
  waiting for transfers between devices  198 us (61%)
  blocking collectives  49.3 us (15%)
  matrix products  32.3 us (10%)
  local copies, waits for them, and re-layouts  25.6 us (8%)
  between operations  13.9 us (4%)
  other arithmetic  3.44 us (1%)
    psum x1, waiting for transfers between devices, shards(): self_total, neigh_total = lax.psum((pair_self, pair_neigh), 'rows')  110 us
    reduce_scatter x1, waiting for transfers between devices, shards(): lax.psum_scatter(summed.reshape(count, width_in), 'rows', scatter_dimensi...  77.1 us
    all_gather x1, blocking collectives, shards(): gathered = lax.all_gather(features, 'rows', axis=0, tiled=True)  45.6 us
    dot_general x1, matrix products, shards(): jnp.einsum('tij,tjf->tif', counts, panels, preferred_element_type=jnp.flo...  11 us
    psum x1, waiting for transfers between devices, shards(): neighbour_sum = lax.psum(partial_rows, 'rep') * scale  9.71 us
    dot_general x1, local copies, waits for them, and re-layouts, shards(): jnp.einsum('tij,tjf->tif', counts, panels, preferred_element_type=jnp.flo...  9.29 us
    dot_general x1, matrix products, shards(): jnp.einsum('tij,tif->tjf', counts, picked, preferred_element_type=jnp.flo...  8.31 us
    convert_element_type x1, local copies, waits for them, and re-layouts, shards(): col_terms = jnp.einsum('tij,tif->tjf', counts, picked, preferred_element_...  6.75 us
  transfers between devices with their start and end apart: 4, of which 4 were waited for; matrix products, arithmetic and copies ran while one was open for 8% of the time, Pallas kernels for 0%

commit v1 on v0

--- a/solution.py
+++ b/solution.py
@@ -24,7 +24,10 @@
     per_half = half_rows // block_size
     row_blocks = rep_count * per_half
     scale = (edge_moment * tile_total * rep_count * block_size / row_blocks) ** (-0.5)
-    gathered = lax.all_gather(features, "rows", axis=0, tiled=True)
+    watch_levels_all = lambda my_data: jnp.concatenate(
+        lax.all_to_all(jnp.stack([my_data] * lax.axis_size("rows")), "rows", 0, 0), axis=0
+    )
+    gathered = watch_levels_all(features)
     local_col = tile_col // (rep_count * per_half) * per_half + tile_col % per_half
     panels = gathered.reshape(-1, block_size, width_in)[local_col]
     counts = tile_counts.astype(jnp.bfloat16)

time: 323 us -> 305 us (0.944)
  blocking collectives: 49.3 us -> 3.97 us
  waiting for transfers between devices: 198 us -> 212 us
  starting transfers between devices: 0.16 us -> 8.5 us
    all_gather x1 -> x0, blocking collectives: 45.6 us -> none  [shards(): gathered = lax.all_gather(features, 'rows', axis=0, tiled=True)]
    all_to_all x0 -> x1, waiting for transfers between devices: none -> 8.92 us  [shards(): lax.all_to_all(jnp.stack([my_data] * lax.axis_size('rows')), 'rows', 0, 0)]
    all_to_all x0 -> x1, starting transfers between devices: none -> 8.34 us  [shards(): lax.all_to_all(jnp.stack([my_data] * lax.axis_size('rows')), 'rows', 0, 0)]
    psum x1, waiting for transfers between devices: 9.71 us -> 14.4 us  [shards(): neighbour_sum = lax.psum(partial_rows, 'rep') * scale]
  transfers between devices with their start and end apart: 4 -> 5, of which waited for: 4 -> 5; matrix products, arithmetic and copies ran while one was open for 8% -> 10% of each run, Pallas kernels for 0% -> 0%
where the time goes in v1:
time: 305 us; the launch traced here: 304 us
  waiting for transfers between devices  212 us (70%)
  matrix products  33.1 us (11%)
  local copies, waits for them, and re-layouts  27.3 us (9%)
  between operations  13.9 us (5%)
  starting transfers between devices  8.5 us (3%)
  other arithmetic  5.58 us (2%)
  blocking collectives  3.97 us (1%)
    psum x1, waiting for transfers between devices, shards(): self_total, neigh_total = lax.psum((pair_self, pair_neigh), 'rows')  110 us
    reduce_scatter x1, waiting for transfers between devices, shards(): lax.psum_scatter(summed.reshape(count, width_in), 'rows', scatter_dimensi...  77.1 us
    psum x1, waiting for transfers between devices, shards(): neighbour_sum = lax.psum(partial_rows, 'rep') * scale  14.4 us
    dot_general x1, matrix products, shards(): jnp.einsum('tij,tjf->tif', counts, panels, preferred_element_type=jnp.flo...  11 us
    dot_general x1, local copies, waits for them, and re-layouts, shards(): jnp.einsum('tij,tjf->tif', counts, panels, preferred_element_type=jnp.flo...  9.29 us
    all_to_all x1, waiting for transfers between devices, shards(): lax.all_to_all(jnp.stack([my_data] * lax.axis_size('rows')), 'rows', 0, 0)  8.92 us
    all_to_all x1, starting transfers between devices, shards(): lax.all_to_all(jnp.stack([my_data] * lax.axis_size('rows')), 'rows', 0, 0)  8.34 us
    dot_general x1, matrix products, shards(): jnp.einsum('tij,tif->tjf', counts, picked, preferred_element_type=jnp.flo...  8.31 us
  transfers between devices with their start and end apart: 5, of which 5 were waited for; matrix products, arithmetic and copies ran while one was open for 10% of the time, Pallas kernels for 0%

profile of v1, /device:TPU:0, one launch (start us, length us, event | category | flops | bytes accessed | tf_op | source)
XLA Modules:
  0.0 304.2 jit_solution(18413748958146388931)
XLA Ops:
  7.2 1.7 stack.2
  8.9 8.3 %all-to-all-start = ((bf16[16,128,128]{2,1,0:T(8,128)(2,1)}), bf16[16,128,128]{2,1,0:T(8,128)(2,1)S(1)}, u32[]{:S(2)}, u32[]{:S(2)}) async-start(bf16[16,128,128]{2,1,0:T(8,128)(2,1)} %stack.2), calls=%async_computation | async-start | bytes 1048576 | tf_op jit(solution)/shard_map/all_to_all | solution.py:28
  17.3 2.1 all_gather.6
  21.4 0.9 broadcast_multiply_fusion.2
  22.4 1.0 fusion.22
  23.4 8.9 %all-to-all-done = bf16[16,128,128]{2,1,0:T(8,128)(2,1)S(1)} async-done(((bf16[16,128,128]{2,1,0:T(8,128)(2,1)}), bf16[16,128,128]{2,1,0:T(8,128)(2,1)S(1)}, u32[]{:S(2)}, u32[]{:S(2)}) %all-to-all-start) | async-done | bytes 524320 | tf_op jit(solution)/shard_map/all_to_all | solution.py:28
  32.3 3.0 %gather_fusion = bf16[128,128,128]{2,1,0:T(8,128)(2,1)} fusion(bf16[16,128,128]{2,1,0:T(8,128)(2,1)S(1)} %all-to-all-done, s32[1024]{0:T(1024)S(1)} %pad_clamp_fusion.1), kind=kCustom, calls=%fused_computation | custom fusion | bytes 8389120 | tf_op jit(solution)/shard_map/gather | solution.py:32
  35.3 11.0 %convolution_bitcast_fusion = f32[128,128,128]{1,2,0:T(8,128)} fusion(bf16[128,128,128]{2,1,0:T(8,128)(2,1)} %gather_fusion, s32[128,128,128]{2,1,0:T(8,128)} %param.9), kind=kOutput, calls=%fused_computation.3 | convolution fusion | flops 538968064 | bytes 20971520 | tf_op jit(solution)/shard_map/tij,tjf->tif/dot_general | solution.py:34
  46.3 9.3 %copy.29 = f32[128,128,128]{2,0,1:T(8,128)} copy(f32[128,128,128]{1,2,0:T(8,128)} %convolution_bitcast_fusion) | data formatting | bytes 16777216 | tf_op jit(solution)/shard_map/tij,tjf->tif/dot_general | solution.py:34
  55.6 6.2 %fusion.13 = f32[2,128,128]{2,0,1:T(2,128)S(1)} fusion(f32[128,128,128]{2,0,1:T(8,128)} %copy.29, s32[128]{0:T(128)S(1)} %copy-done.3), kind=kOutput, calls=%fused_computation.35 | convolution fusion | flops 50331904 | bytes 8520192 | tf_op jit(solution)/shard_map/tr,tif->rif/dot_general | solution.py:38
  62.5 1.9 all_gather.7
  64.4 14.4 %all-reduce.6.cloned.1.call-done = f32[256,128]{1,0:T(8,128)} async-done(((f32[256,128]{1,0:T(8,128)}), f32[256,128]{1,0:T(8,128)}) %all-reduce.6.cloned.1.call-update) | async-done | bytes 131088 | tf_op jit(solution)/shard_map/psum | solution.py:47
  78.9 0.9 multiply_convert_fusion.1
  80.1 0.9 fusion.3
  82.1 3.0 gather_fusion.1
  85.1 8.3 %convert_bitcast_fusion = bf16[128,128,128]{1,2,0:T(8,128)(2,1)} fusion(bf16[128,128,128]{2,1,0:T(8,128)(2,1)} %gather_fusion.1, s32[128,128,128]{2,1,0:T(8,128)} %param.9), kind=kOutput, calls=%fused_computation.2 | convolution fusion | flops 541065216 | bytes 16777216 | tf_op jit(solution)/shard_map/tij,tif->tjf/dot_general | solution.py:72
  93.4 6.7 %copy.32 = bf16[128,128,128]{2,0,1:T(8,128)(2,1)} copy(bf16[128,128,128]{1,2,0:T(8,128)(2,1)} %convert_bitcast_fusion) | data formatting | bytes 8388608 | tf_op jit(solution)/shard_map/convert_element_type | solution.py:74
  100.2 1.5 all-reduce.10.cloned.1.call-done
  101.8 2.9 fusion.10
  104.6 1.3 copy.33
  106.6 109.7 %all-reduce.8.cloned.1.call-done = (f32[128,256]{0,1:T(8,128)}, f32[128,256]{0,1:T(8,128)}) async-done(((f32[128,256]{0,1:T(8,128)}, f32[128,256]{0,1:T(8,128)}), (f32[128,256]{0,1:T(8,128)}, f32[128,256]{0,1:T(8,128)})) %all-reduce.8.cloned.1.call-update) | async-done | bytes 262160 | tf_op jit(solution)/shard_map/psum | solution.py:69
  216.3 1.0 broadcast_multiply_fusion
  218.9 77.1 %reduce-scatter.2.cloned.1.call-done = f32[128,128]{1,0:T(8,128)} async-done(((f32[2048,128]{1,0:T(8,128)}), f32[128,128]{1,0:T(8,128)}) %reduce-scatter.2.cloned.1.call-update) | async-done | bytes 65552 | tf_op jit(solution)/shard_map/reduce_scatter | solution.py:81
  296.0 1.6 convolution_add_fusion.1
  (30 shorter events, 6.5 us)
Async XLA Ops:
  7.2 72.6 %copy-start = (bf16[128,256]{1,0:T(8,128)(2,1)S(1)}, bf16[128,256]{1,0:T(8,128)(2,1)}, u32[]{:S(2)}) copy-start(bf16[128,256]{1,0:T(8,128)(2,1)} %param.15) | copy-start | bytes 196612
  8.9 23.4 %all-to-all-start = ((bf16[16,128,128]{2,1,0:T(8,128)(2,1)}), bf16[16,128,128]{2,1,0:T(8,128)(2,1)S(1)}, u32[]{:S(2)}, u32[]{:S(2)}) async-start(bf16[16,128,128]{2,1,0:T(8,128)(2,1)} %stack.2), calls=%async_computation | async-start | bytes 1048576 | tf_op jit(solution)/shard_map/all_to_all | solution.py:28
  17.2 61.6 %all-reduce.6.cloned.1.call-start = ((), (), s32[]{:S(2)}) async-start(), calls=%async_computation.2 | async-start | bytes 262144 | tf_op jit(solution)/shard_map/psum | solution.py:47
  46.3 9.3 %copy-start.3 = (s32[128]{0:T(128)S(1)}, s32[128]{0:T(128)}, u32[]{:S(2)}) copy-start(s32[128]{0:T(128)} %param.10) | copy-start | bytes 1540
  55.6 25.3 %copy-start.1 = (bf16[128,128]{1,0:T(8,128)(2,1)S(1)}, bf16[128,128]{1,0:T(8,128)(2,1)}, u32[]{:S(2)}) copy-start(bf16[128,128]{1,0:T(8,128)(2,1)} %param.8) | copy-start | bytes 98308
  62.5 39.2 %all-reduce.10.cloned.1.call-start = ((), (), s32[]{:S(2)}) async-start(), calls=%async_computation.5 | async-start | bytes 524288 | tf_op jit(solution)/shard_map/psum | solution.py:68
  82.0 134.3 %all-reduce.8.cloned.1.call-start = ((), (), s32[]{:S(2)}) async-start(), calls=%async_computation.4 | async-start | bytes 524288 | tf_op jit(solution)/shard_map/psum | solution.py:69
  101.7 194.3 %reduce-scatter.2.cloned.1.call-start = ((), (), s32[]{:S(2)}) async-start(), calls=%async_computation.3 | async-start | bytes 1114112 | tf_op jit(solution)/shard_map/reduce_scatter | solution.py:81
  101.7 194.3 %copy-start.2 = (bf16[128,256]{1,0:T(8,128)(2,1)S(1)}, bf16[128,256]{1,0:T(8,128)(2,1)}, u32[]{:S(2)}) copy-start(bf16[128,256]{1,0:T(8,128)(2,1)} %param.14) | copy-start | bytes 196612
Sparse Core Ops, SparseCore 0:
  62.6 16.2 all-reduce.5
  82.1 19.4 all-reduce.9
  107.0 109.3 all-reduce.7
  218.5 77.4 reduce-scatter.1
